TPU v7x, 32 devices: a whole 2x2x4 slice. The times are simulated.
32 devices in a mesh: wide: 8 (over z, core), narrow: 4 (over y, x).
Axes of the slice: x: 2, y: 2, z: 4, core: 2. Of those that a mesh axis runs over, the one named last changes fastest.
Arguments:
- amplitudes: float32 [4, 64, 640, 640], P(None, 'wide', None, 'narrow'), may hold values from -6 to 6
- cycle_block: float32 [64, 640, 4, 640], P('wide', 'narrow'), may hold values from -0.078125 to 0.078125
- occupied_irreps: int32 [64], replicated, may hold values from 0 to 7, as said below
- virtual_irreps: int32 [640], replicated, may hold values from 0 to 7, as said below
- slab_orbitals: int32 [4], replicated, may hold values from 0 to 63, as said below
Outputs:
- cycle_residual: float32 [4, 4, 640, 640], P(None, None, 'narrow', 'wide')
Inputs may be any that keep to these rules, and one draw needn't show every extreme that they name: `occupied_irreps`: nondecreasing; every irrep 0 to 7 labels at least 4 orbitals. `virtual_irreps`: nondecreasing; every irrep 0 to 7 labels at least 64 orbitals. `slab_orbitals`: distinct occupied orbital indices in increasing order; the last is 63.
All inputs are finite; a program needn't handle non-finite values.
Results may differ from a plain program's by a relative error of at most 0.0003.
Values sent between devices are 32-bit elements; how exact they have to be, the bound alone decides.
A program may use at most 192 MiB of HBM per device.

v0:
```python
import jax
import jax.numpy as jnp
from jax import lax
from jax.sharding import PartitionSpec as P


def select_sym(values, first, second, third, fourth):
    labels = jnp.bitwise_xor(
        jnp.bitwise_xor(first[:, None, None, None], second[None, :, None, None]),
        jnp.bitwise_xor(third[None, None, :, None], fourth[None, None, None, :]),
    )
    return jnp.where(labels == 0, values, jnp.zeros_like(values))


def local(amplitudes, cycle_block, occupied_irreps, virtual_irreps, slab_orbitals):
    occ_local = amplitudes.shape[1]
    vir_all = amplitudes.shape[2]
    vir_local = amplitudes.shape[3]
    orbits = jnp.arange(occupied_irreps.shape[0], dtype=jnp.int32)
    slab_irreps = jnp.sum(
        jnp.where(orbits[None, :] == slab_orbitals[:, None], occupied_irreps[None, :], 0), axis=1
    )
    wide_pos = lax.axis_index("wide")
    narrow_pos = lax.axis_index("narrow")
    occ_part = lax.dynamic_slice_in_dim(occupied_irreps, wide_pos * occ_local, occ_local)
    vir_part = lax.dynamic_slice_in_dim(virtual_irreps, narrow_pos * vir_local, vir_local)
    kept_amps = select_sym(amplitudes, slab_irreps, occ_part, virtual_irreps, vir_part)
    kept_cycle = select_sym(cycle_block, occ_part, vir_part, slab_irreps, virtual_irreps)
    regrouped = lax.all_to_all(kept_amps, "narrow", split_axis=2, concat_axis=3, tiled=True)
    partial_value = jnp.einsum(
        "ikac,kcjb->iajb",
        regrouped,
        lax.all_gather(kept_cycle, "narrow", axis=1, tiled=True),
        precision=lax.Precision.HIGHEST,
    )
    summed = lax.psum(partial_value, "wide")
    b_width = vir_all // lax.axis_size("wide")
    owned = lax.dynamic_slice_in_dim(summed, wide_pos * b_width, b_width, 3)
    return jnp.transpose(owned, (0, 2, 1, 3))


def solution(mesh):
    placed = (P(None, "wide", None, "narrow"), P("wide", "narrow", None, None), P(), P(), P())
    return jax.shard_map(
        local,
        mesh=mesh,
        in_specs=placed,
        out_specs=P(None, None, "narrow", "wide"),
        check_vma=False,
    )
```

profile of v0, /device:TPU:0, one launch (start us, length us, event | category | flops | bytes accessed | tf_op | source)
XLA Modules:
  0.0 985.0 jit_solution(12330437346544218026)
XLA Ops:
  6.5 0.0 all-gather.2.cloned.1.call-start
  6.5 0.7 dynamic_slice.9
  7.3 0.9 select_reduce_fusion
  8.1 0.8 dynamic_slice.10
  8.9 0.8 broadcast_xor_fusion.1
  9.6 0.1 broadcast_xor_fusion.2
  9.7 10.9 %copy_select_fusion = f32[8,160,4,640]{3,1,0,2:T(8,128)} fusion(f32[8,160,4,640]{3,2,1,0:T(4,128)} %param.6, s32[4,640]{1,0:T(4,128)S(1)} %broadcast_xor_fusion.1, s32[8,160]{1,0:T(8,128)S(1)} %broadcast_xor_fusion.2), kind=kLoop, calls=%fused_computation.6 | loop fusion | flops 9830400 | bytes 26229760 | tf_op jit(solution)/shard_map/jit(_where)/select_n | solution.py:12
  20.6 0.0 all-gather.2.cloned.1.call-update
  20.7 0.0 copy-start
  20.7 0.0 all-reduce.2.cloned.1.call-start
  20.7 24.0 %copy.11 = f32[4,8,640,160]{3,1,0,2:T(8,128)} copy(f32[4,8,640,160]{2,3,1,0:T(8,128)} %param.5) | data formatting | bytes 26214400 | tf_op args[0]
  44.7 0.1 broadcast_xor_fusion.3
  44.8 0.0 copy-done
  44.8 0.1 broadcast_xor_fusion
  45.0 13.1 %fusion.2 = f32[4,8,640,160]{3,1,0,2:T(8,128)S(1)} fusion(f32[4,8,640,160]{3,1,0,2:T(8,128)} %copy.11, s32[640,160]{1,0:T(8,128)S(1)} %broadcast_xor_fusion, s32[4,8]{1,0:T(4,128)S(1)} %broadcast_xor_fusion.3), kind=kLoop, calls=%fused_computation.4 | loop fusion | flops 9830400 | bytes 26624128 | tf_op jit(solution)/shard_map/jit(_where)/select_n | solution.py:12
  58.1 356.7 %all_to_all.18 = f32[4,8,640,160]{3,1,0,2:T(8,128)} all-to-all(f32[4,8,640,160]{3,1,0,2:T(8,128)S(1)} %fusion.2), channel_id=1, replica_groups=mesh['wide'=8,'narrow'=4] {'narrow'}, dimensions={2} | all-to-all | bytes 26214400 | tf_op jit(solution)/shard_map/all_to_all | solution.py:29
  414.8 27.2 %copy.18 = f32[4,8,4,160,160]{4,2,3,1,0:T(4,128)} copy(f32[4,8,4,160,160]{4,1,0,3,2:T(8,128)} %bitcast.19) | data formatting | bytes 26214400 | tf_op jit(solution)/shard_map/all_to_all | solution.py:29
  442.0 21.7 %reshape.130 = f32[4,8,160,640,1]{3,2,1,0,4:T(8,128)} reshape(f32[4,8,160,4,160]{4,3,2,1,0:T(4,128)} %bitcast.20) | data formatting | bytes 26214400 | tf_op jit(solution)/shard_map/all_to_all | solution.py:29
  463.8 239.7 %all-gather.2.cloned.1.call-done = f32[8,640,4,640]{3,1,0,2:T(8,128)} async-done(((f32[8,160,4,640]{3,1,0,2:T(8,128)}), f32[8,640,4,640]{3,1,0,2:T(8,128)}) %all-gather.2.cloned.1.call-update) | async-done | bytes 52428816 | tf_op jit(solution)/shard_map/all_gather | solution.py:33
  703.5 130.4 %fusion.4 = f32[4,160,4,640]{3,1,2,0:T(8,128)} fusion(f32[8,640,4,640]{3,1,0,2:T(8,128)} %all-gather.2.cloned.1.call-done, f32[4,8,160,640,1]{3,2,1,0,4:T(8,128)} %reshape.130), kind=kOutput, calls=%fused_computation.8 | convolution fusion | flops 100663296000 | bytes 72089600 | tf_op jit(solution)/shard_map/ikac,kcjb->iajb/dot_general | solution.py:30
  833.8 0.0 all-reduce.2.cloned.1.call-update
  833.9 141.1 %all-reduce.2.cloned.1.call-done = f32[4,160,4,640]{3,1,2,0:T(8,128)} async-done(((f32[4,160,4,640]{3,1,2,0:T(8,128)}), f32[4,160,4,640]{3,1,2,0:T(8,128)}) %all-reduce.2.cloned.1.call-update) | async-done | bytes 6553616 | tf_op jit(solution)/shard_map/psum | solution.py:36
  975.0 3.2 dynamic-slice_bitcast_fusion
Async XLA Ops:
  6.5 697.0 %all-gather.2.cloned.1.call-start = ((), (), s32[]{:S(2)}) async-start(), calls=%async_computation.1 | async-start | bytes 65536000 | tf_op jit(solution)/shard_map/all_gather | solution.py:33
  20.7 24.2 %copy-start = (s32[640]{0:T(1024)S(1)}, s32[640]{0:T(1024)}, u32[]{:S(2)}) copy-start(s32[640]{0:T(1024)} %param.8) | copy-start | bytes 7684
  20.7 954.3 %all-reduce.2.cloned.1.call-start = ((), (), s32[]{:S(2)}) async-start(), calls=%async_computation.2 | async-start | bytes 13107200 | tf_op jit(solution)/shard_map/psum | solution.py:36
Sparse Core Ops, SparseCore 0:
  20.8 682.6 all-gather.1
  834.0 140.9 all-reduce.1
where the time goes:
time: 986 us; the launch traced here: 985 us
  waiting for transfers between devices  381 us (39%)
  blocking collectives  357 us (36%)
  matrix products  130 us (13%)
  local copies, waits for them, and re-layouts  77.6 us (8%)
  other arithmetic  26 us (3%)
  between operations  13.4 us (1%)
    all_to_all x1, blocking collectives, local(): lax.all_to_all(kept_amps, 'narrow', split_axis=2, concat_axis=3, tiled=True)  357 us
    all_gather x1, waiting for transfers between devices, local(): lax.all_gather(kept_cycle, 'narrow', axis=1, tiled=True)  240 us
    psum x1, waiting for transfers between devices, local(): summed = lax.psum(partial_value, 'wide')  141 us
    dot_general x1, matrix products, local(): jnp.einsum('ikac,kcjb->iajb', regrouped, lax.all_gather(kept_cycle, 'narr...  130 us
    all_to_all x2, local copies, waits for them, and re-layouts, local(): lax.all_to_all(kept_amps, 'narrow', split_axis=2, concat_axis=3, tiled=True)  48.9 us
    select_n x2, other arithmetic, select_sym(): return jnp.where(labels == 0, values, jnp.zeros_like(values))  24.1 us
    unnamed x3, local copies, waits for them, and re-layouts  24 us
  transfers between devices with their start and end apart: 2, of which 2 were waited for; matrix products, arithmetic and copies ran while one was open for 9% of the time, Pallas kernels for 0%

commit v1 on v0

v1 whole, which is shorter than its diff:
```python
import functools

import jax
import jax.numpy as jnp
from jax import lax
from jax.experimental import pallas as pl
from jax.experimental.pallas import tpu as pltpu
from jax.sharding import PartitionSpec as P

IRREPS = 8
ROWS = 8
FEWEST = 64


def split(x):
    high = x.astype(jnp.bfloat16)
    low = (x - high.astype(jnp.float32)).astype(jnp.bfloat16)
    return high, low


def mm(x, y):
    return jnp.dot(x, y, preferred_element_type=jnp.float32)


def contract(cap, wide, tab, a_ref, w_ref, hc_row, hc_col, hb_row, out_ref, acc, rows):
    k = pl.program_id(0)
    n_k = pl.num_programs(0)
    ni = a_ref.shape[0]
    nb = w_ref.shape[3]
    bw = nb // wide
    hk = tab[ni + k]
    base = ni + n_k
    first, last = tab[base + IRREPS], tab[base + IRREPS + 1]
    c_labels = hc_row[...]
    for i in range(ni):
        g = tab[i] ^ hk

        def pick(h, kept):
            block = a_ref[i, 0, pl.ds(pl.multiple_of(tab[base + (h ^ g)], ROWS), cap), :]
            return jnp.where(c_labels == h, block, kept)

        rows[i * cap : (i + 1) * cap, :] = lax.fori_loop(
            first, last + 1, pick, jnp.zeros((cap, a_ref.shape[3]), jnp.float32)
        )
    l_hi, l_lo = split(rows[...])
    labels = hc_col[...] ^ hb_row[...]
    w_all = jnp.swapaxes(w_ref[0], 0, 1)
    for j in range(ni):
        w = jnp.where(labels == (tab[j] ^ hk), w_all[j], 0.0)
        w_hi, w_lo = split(w)
        term = mm(l_hi, w_hi) + mm(l_hi, w_lo) + mm(l_lo, w_hi)

        @pl.when(k == 0)
        def _():
            acc[j] = term

        @pl.when(k > 0)
        def _():
            acc[j] += term

    @pl.when(k == n_k - 1)
    def _():
        for j in range(ni):
            turned = acc[j].T
            for w in range(wide):
                out_ref[(w * ni + j) * bw : (w * ni + j + 1) * bw, :] = turned[w * bw : (w + 1) * bw]


def unpack(cap, tab, g_ref, hb_row, out_ref, buf):
    ni, _, na, bw = out_ref.shape
    buf[...] = jnp.zeros_like(buf)
    first, last, a0 = (tab[ni + 3 * IRREPS + n] for n in range(3))
    labels = hb_row[...]
    at = a0 + lax.broadcasted_iota(jnp.int32, (na, bw), 0)
    for j in range(ni):
        turned = g_ref[j * bw : (j + 1) * bw, :].T
        for i in range(ni):
            buf[na : na + cap, :] = turned[i * cap : (i + 1) * cap]
            g = tab[i] ^ tab[j]

            def place(h, kept):
                block = h ^ g
                start = jnp.clip(na + a0 - tab[ni + block], 0, na + cap)
                low, high = tab[ni + IRREPS + block], tab[ni + 2 * IRREPS + block]
                use = (labels == h) & (at >= low) & (at < high)
                return jnp.where(use, buf[pl.ds(pl.multiple_of(start, ROWS), na), :], kept)

            out_ref[i, j] = lax.fori_loop(first, last + 1, place, jnp.zeros((na, bw), jnp.float32))


def local(amplitudes, cycle_block, occupied_irreps, virtual_irreps, slab_orbitals):
    ni, n_k, va, nc = amplitudes.shape
    vb = cycle_block.shape[3]
    wide, narrow = lax.axis_size("wide"), lax.axis_size("narrow")
    wide_pos, narrow_pos = lax.axis_index("wide"), lax.axis_index("narrow")
    bw, na = vb // wide, va // narrow
    most = va - (IRREPS - 1) * FEWEST
    cap = most // 2

    slab = jnp.sum(
        jnp.where(
            jnp.arange(occupied_irreps.shape[0], dtype=jnp.int32)[None, :] == slab_orbitals[:, None],
            occupied_irreps[None, :],
            0,
        ),
        axis=1,
    )
    occ_part = lax.dynamic_slice_in_dim(occupied_irreps, wide_pos * n_k, n_k)
    c_part = lax.dynamic_slice_in_dim(virtual_irreps, narrow_pos * nc, nc)
    b_part = lax.dynamic_slice_in_dim(virtual_irreps, wide_pos * bw, bw)
    names = jnp.arange(IRREPS, dtype=jnp.int32)
    starts = jnp.sum((virtual_irreps[None, :] < names[:, None]).astype(jnp.int32), axis=1)
    aligned = starts // ROWS * ROWS
    ends = jnp.concatenate([starts[1:], jnp.full((1,), va, jnp.int32)])

    def part(offset):
        packed = jnp.minimum(aligned + offset, va - cap)
        tab = jnp.concatenate([slab, occ_part, packed, c_part[:1], c_part[-1:]])
        partial_sums = pl.pallas_call(
            functools.partial(contract, cap, wide),
            out_shape=jax.ShapeDtypeStruct((ni * vb, ni * cap), jnp.float32),
            grid_spec=pltpu.PrefetchScalarGridSpec(
                num_scalar_prefetch=1,
                grid=(n_k,),
                in_specs=[
                    pl.BlockSpec((ni, 1, va, nc), lambda k, t: (0, k, 0, 0)),
                    pl.BlockSpec((1, nc, ni, vb), lambda k, t: (k, 0, 0, 0)),
                    pl.BlockSpec((1, nc), lambda k, t: (0, 0)),
                    pl.BlockSpec((nc, 1), lambda k, t: (0, 0)),
                    pl.BlockSpec((1, vb), lambda k, t: (0, 0)),
                ],
                out_specs=pl.BlockSpec((ni * vb, ni * cap), lambda k, t: (0, 0)),
                scratch_shapes=[
                    pltpu.VMEM((ni, ni * cap, vb), jnp.float32),
                    pltpu.VMEM((ni * cap, nc), jnp.float32),
                ],
            ),
            compiler_params=pltpu.CompilerParams(vmem_limit_bytes=60 * 2**20),
        )(tab, amplitudes, cycle_block, c_part[None, :], c_part[:, None], virtual_irreps[None, :])
        mine = lax.psum_scatter(partial_sums, ("wide", "narrow"), scatter_dimension=0, tiled=True)
        summed = lax.all_gather(mine, "narrow", axis=0, tiled=True)
        low = jnp.maximum(aligned + offset, starts)
        high = jnp.minimum(aligned + offset + cap, ends)
        tab = jnp.concatenate([slab, packed, low, high, b_part[:1], b_part[-1:], (narrow_pos * na)[None]])
        return pl.pallas_call(
            functools.partial(unpack, cap),
            out_shape=jax.ShapeDtypeStruct((ni, ni, na, bw), jnp.float32),
            grid_spec=pltpu.PrefetchScalarGridSpec(
                num_scalar_prefetch=1,
                grid=(1,),
                in_specs=[
                    pl.BlockSpec((ni * bw, ni * cap), lambda k, t: (0, 0)),
                    pl.BlockSpec((1, bw), lambda k, t: (0, 0)),
                ],
                out_specs=pl.BlockSpec((ni, ni, na, bw), lambda k, t: (0, 0, 0, 0)),
                scratch_shapes=[pltpu.VMEM((2 * na + cap, bw), jnp.float32)],
            ),
        )(tab, summed, b_part[None, :])

    first = part(0)
    return lax.cond(jnp.max(ends - aligned) > cap, lambda x: x + part(cap), lambda x: x, first)


def solution(mesh):
    placed = (P(None, "wide", None, "narrow"), P("wide", "narrow", None, None), P(), P(), P())
    return jax.shard_map(
        local,
        mesh=mesh,
        in_specs=placed,
        out_specs=P(None, None, "narrow", "wide"),
        check_vma=False,
    )
```

time: 986 us -> 211 us (0.21)
  blocking collectives: 357 us -> 11.7 us
  waiting for transfers between devices: 381 us -> 104 us
  matrix products: 130 us -> 0 us
  Pallas kernels: 0 us -> 48.6 us
  local copies, waits for them, and re-layouts: 77.6 us -> 30.2 us
  other arithmetic: 26 us -> 2.45 us
    all_to_all x1 -> x0, blocking collectives: 357 us -> none  [local(): lax.all_to_all(kept_amps, 'narrow', split_axis=2, concat_axis=3, tiled=True)]
    all_gather x1 -> x0, waiting for transfers between devices: 240 us -> none  [local(): lax.all_gather(kept_cycle, 'narrow', axis=1, tiled=True)]
    psum x1 -> x0, waiting for transfers between devices: 141 us -> none  [local(): summed = lax.psum(partial_value, 'wide')]
    dot_general x1 -> x0, matrix products: 130 us -> none  [local(): jnp.einsum('ikac,kcjb->iajb', regrouped, lax.all_gather(kept_cycle, 'narr...]
    reduce_scatter x0 -> x1, waiting for transfers between devices: none -> 104 us  [part(): lax.psum_scatter(partial_sums, ('wide', 'narrow'), scatter_dimension=0, t...]
    all_to_all x2 -> x0, local copies, waits for them, and re-layouts: 48.9 us -> none  [local(): lax.all_to_all(kept_amps, 'narrow', split_axis=2, concat_axis=3, tiled=True)]
    pallas_call x0 -> x2, Pallas kernels: none -> 48.6 us  [the longest x1 45.8 us: part(): pl.pallas_call(functools.partial(contract, cap, wide), out_shape=jax.Shap...]
    select_n x2 -> x0, other arithmetic: 24.1 us -> none  [select_sym(): return jnp.where(labels == 0, values, jnp.zeros_like(values))]
  transfers between devices with their start and end apart: 2 -> 1, of which waited for: 2 -> 1; matrix products, arithmetic and copies ran while one was open for 9% -> 2% of each run, Pallas kernels for 0% -> 0%
where the time goes in v1:
time: 211 us
  waiting for transfers between devices  104 us (49%)
  Pallas kernels  48.6 us (23%)
  local copies, waits for them, and re-layouts  30.2 us (14%)
  between operations  14.1 us (7%)
  blocking collectives  11.7 us (6%)
  other arithmetic  2.45 us (1%)
    reduce_scatter x1, waiting for transfers between devices, part(): lax.psum_scatter(partial_sums, ('wide', 'narrow'), scatter_dimension=0, t...  104 us
    pallas_call x1, Pallas kernels, part(): pl.pallas_call(functools.partial(contract, cap, wide), out_shape=jax.Shap...  45.8 us
    unnamed x5, local copies, waits for them, and re-layouts  20.8 us
    all_gather x1, blocking collectives, part(): summed = lax.all_gather(mine, 'narrow', axis=0, tiled=True)  11.7 us
  transfers between devices with their start and end apart: 1, of which 1 were waited for; matrix products, arithmetic and copies ran while one was open for 2% of the time, Pallas kernels for 0%

profile of v1, /device:TPU:0, one launch (start us, length us, event | category | flops | bytes accessed | tf_op | source)
XLA Modules:
  0.0 210.6 jit_solution(9640255009092216787)
XLA Ops:
  6.5 0.0 reduce-scatter.5.cloned.1.call-start
  6.5 0.8 convert_reduce_fusion
  7.3 1.3 broadcast_in_dim.52.hb_row
  8.6 0.8 dynamic_slice.11
  9.4 0.7 dynamic_slice.10
  10.1 0.9 select_reduce_fusion
  11.0 0.1 slice.27
  11.0 0.7 fusion.4
  11.7 0.1 add_minimum_fusion.2
  11.8 0.7 pad_add_fusion
  12.5 0.8 copy.16.hc_col
  13.2 19.1 %copy.15.a_ref = f32[4,8,640,160]{3,2,1,0:T(8,128)} copy(f32[4,8,640,160]{2,3,1,0:T(8,128)} %param.7) | data formatting | bytes 26214400 | tf_op args[0]
  32.3 2.0 concatenate.17.tab
  34.3 45.8 %shard_map.57 = f32[2560,384]{1,0:T(8,128)} custom-call(s32[22]{0:T(128)} %concatenate.17.tab, f32[4,8,640,160]{3,2,1,0:T(8,128)} %copy.15.a_ref, f32[8,160,4,640]{3,2,1,0:T(4,128)} %w_ref.1, s32[1,160]{1,0:T(1,128)S(1)} %bitcast.10, s32[160,1]{1,0:T(8,128)} %copy.16.hc_col, s32[1,640]{1,0:T(1,128)} %broadcast_in_dim.52.hb_row), custom_call_target="tpu_custom_call" | custom-call | tf_op jit(solution)/shard_map/pallas_call | solution.py:119
  80.1 0.0 copy-start.1
  80.1 0.0 reduce-scatter.5.cloned.1.call-update
  80.1 0.7 copy-done.1
  80.8 0.1 dynamic_slice.9
  81.5 0.6 fusion.5
  82.1 2.0 concatenate.16.tab
  84.0 0.6 dynamic-slice_bitcast_fusion.hb_row
  84.6 103.5 %reduce-scatter.5.cloned.1.call-done = f32[80,384]{1,0:T(8,128)} async-done(((f32[2560,384]{1,0:T(8,128)}), f32[80,384]{1,0:T(8,128)}) %reduce-scatter.5.cloned.1.call-update) | async-done | bytes 122896 | tf_op jit(solution)/shard_map/reduce_scatter | solution.py:140
  188.1 11.7 %all_gather.6.g_ref = f32[320,384]{1,0:T(8,128)} all-gather(f32[80,384]{1,0:T(8,128)} %reduce-scatter.5.cloned.1.call-done), channel_id=1, replica_groups=mesh['wide'=8,'narrow'=4] {'narrow'}, dimensions={0}, use_global_device_ids=true | all-gather | bytes 614400 | tf_op jit(solution)/shard_map/all_gather | solution.py:141
  199.8 2.8 %shard_map.58 = f32[4,4,160,80]{3,2,1,0:T(8,128)S(1)} custom-call(s32[31]{0:T(128)} %concatenate.16.tab, f32[320,384]{1,0:T(8,128)} %all_gather.6.g_ref, s32[1,80]{1,0:T(1,128)} %dynamic-slice_bitcast_fusion.hb_row), custom_call_target="tpu_custom_call" | custom-call | tf_op jit(solution)/shard_map/pallas_call | solution.py:145
  202.7 0.0 copy-start
  202.7 1.0 copy-done
  (1 shorter events, 0.0 us)
Async XLA Ops:
  6.5 181.6 %reduce-scatter.5.cloned.1.call-start = ((), (), s32[]{:S(2)}) async-start(), calls=%async_computation.3 | async-start | bytes 4055040 | tf_op jit(solution)/shard_map/reduce_scatter | solution.py:140
  80.1 0.7 copy-start.1
  202.7 1.1 copy-start
Sparse Core Ops, SparseCore 0:
  80.2 107.8 reduce-scatter.4

commit v2 on v1

--- a/solution.py
+++ b/solution.py
@@ -8,6 +8,8 @@
 from jax.sharding import PartitionSpec as P
 
 IRREPS = 8
+CORES = 2
+LANES = 128
 ROWS = 8
 FEWEST = 64
 
@@ -22,33 +24,41 @@
     return jnp.dot(x, y, preferred_element_type=jnp.float32)
 
 
-def contract(cap, wide, tab, a_ref, w_ref, hc_row, hc_col, hb_row, out_ref, acc, rows):
+def contract(cap, tab, a_ref, w_ref, hc_row, hc_col, hb_row, out_ref, acc, turn, rows, deep_l, deep_w):
     k = pl.program_id(0)
     n_k = pl.num_programs(0)
-    ni = a_ref.shape[0]
-    nb = w_ref.shape[3]
-    bw = nb // wide
+    ni, nc = a_ref.shape[0], a_ref.shape[2]
+    cores, zs, narrow, nr, _ = out_ref.shape
     hk = tab[ni + k]
     base = ni + n_k
     first, last = tab[base + IRREPS], tab[base + IRREPS + 1]
     c_labels = hc_row[...]
     for i in range(ni):
         g = tab[i] ^ hk
+        turn[i] = a_ref[i, 0].T
 
         def pick(h, kept):
-            block = a_ref[i, 0, pl.ds(pl.multiple_of(tab[base + (h ^ g)], ROWS), cap), :]
-            return jnp.where(c_labels == h, block, kept)
-
-        rows[i * cap : (i + 1) * cap, :] = lax.fori_loop(
-            first, last + 1, pick, jnp.zeros((cap, a_ref.shape[3]), jnp.float32)
-        )
+            start = pl.multiple_of(tab[base + (h ^ g)], ROWS)
+            return jnp.where(c_labels == h, turn[i, pl.ds(start, cap), :], kept)
+
+        rows[i * cap : (i + 1) * cap, :] = lax.fori_loop(first, last + 1, pick, jnp.zeros((cap, nc), jnp.float32))
     l_hi, l_lo = split(rows[...])
+    joined = nc % 16 == 0
+    if joined:
+        deep_l[:, :nc] = l_hi
+        deep_l[:, nc : 2 * nc] = l_hi
+        deep_l[:, 2 * nc :] = l_lo
     labels = hc_col[...] ^ hb_row[...]
     w_all = jnp.swapaxes(w_ref[0], 0, 1)
     for j in range(ni):
-        w = jnp.where(labels == (tab[j] ^ hk), w_all[j], 0.0)
-        w_hi, w_lo = split(w)
-        term = mm(l_hi, w_hi) + mm(l_hi, w_lo) + mm(l_lo, w_hi)
+        w_hi, w_lo = split(jnp.where(labels == (tab[j] ^ hk), w_all[j], 0.0))
+        if joined:
+            deep_w[j, :nc] = w_hi
+            deep_w[j, nc : 2 * nc] = w_lo
+            deep_w[j, 2 * nc :] = w_hi
+            term = mm(deep_l[...], deep_w[j])
+        else:
+            term = mm(l_hi, w_hi) + mm(l_hi, w_lo) + mm(l_lo, w_hi)
 
         @pl.when(k == 0)
         def _():
@@ -60,10 +70,76 @@
 
     @pl.when(k == n_k - 1)
     def _():
+        pieces = narrow // ni
         for j in range(ni):
             turned = acc[j].T
-            for w in range(wide):
-                out_ref[(w * ni + j) * bw : (w * ni + j + 1) * bw, :] = turned[w * bw : (w + 1) * bw]
+            for n in range(cores * zs * pieces):
+                w, piece = divmod(n, pieces)
+                out_ref[w % cores, w // cores, j * pieces + piece] = turned[n * nr : (n + 1) * nr]
+
+
+def exchange(q_ref, out_ref, cbuf, s1, nbuf, s2, zbuf, gbuf, csem, nsend, nrecv, zsend, zrecv, gsend, grecv):
+    cores, zs, narrow, _, lanes = q_ref.shape
+    wide_pos, n = lax.axis_index("wide"), lax.axis_index("narrow")
+    z, core = wide_pos // cores, lax.rem(wide_pos, cores)
+    other = 1 - core
+    partner = (z * cores + other, n)
+    n_peers = [lax.rem(n + d, narrow) for d in range(1, narrow)]
+    z_peers = [lax.rem(z + d, zs) for d in range(1, zs)]
+
+    def at_n(p):
+        return (wide_pos, p)
+
+    def at_z(p):
+        return (p * cores + core, n)
+
+    barrier = pltpu.get_barrier_semaphore()
+    peers = [partner] + [at_n(p) for p in n_peers] + [at_z(p) for p in z_peers]
+    for peer in peers:
+        pl.semaphore_signal(barrier, inc=1, device_id=peer, device_id_type=pl.DeviceIdType.MESH)
+    pl.semaphore_wait(barrier, len(peers))
+
+    def copy(src, dst, send, recv, device):
+        return pltpu.make_async_remote_copy(
+            src_ref=src, dst_ref=dst, send_sem=send, recv_sem=recv, device_id=device, device_id_type=pl.DeviceIdType.MESH
+        )
+
+    groups = [(g, pl.ds(g * LANES, LANES)) for g in range(lanes // LANES)]
+    sent = []
+
+    def push(c):
+        c.start()
+        sent.append(c)
+
+    for g, part in groups:
+        push(copy(q_ref.at[other, :, :, :, part], cbuf.at[:, :, :, part], csem.at[0, g], csem.at[1, g], partner))
+    for g, part in groups:
+        sent[g].wait_recv()
+        s1[:, :, :, part] = q_ref[core, :, :, :, part] + cbuf[:, :, :, part]
+        for p in n_peers:
+            push(copy(s1.at[:, p, :, part], nbuf.at[n, :, :, part], nsend.at[p, g], nrecv.at[n, g], at_n(p)))
+    for g, part in groups:
+        total = s1[:, n, :, part]
+        for p in n_peers:
+            copy(s1.at[:, p, :, part], nbuf.at[p, :, :, part], nsend.at[p, g], nrecv.at[p, g], at_n(p)).wait_recv()
+            total = total + nbuf[p, :, :, part]
+        s2[:, :, part] = total
+        for p in z_peers:
+            push(copy(s2.at[p, :, part], zbuf.at[z, :, part], zsend.at[p, g], zrecv.at[z, g], at_z(p)))
+    for g, part in groups:
+        total = s2[z, :, part]
+        for p in z_peers:
+            copy(s2.at[p, :, part], zbuf.at[p, :, part], zsend.at[p, g], zrecv.at[p, g], at_z(p)).wait_recv()
+            total = total + zbuf[p, :, part]
+        gbuf[n, :, part] = total
+        for p in n_peers:
+            push(copy(gbuf.at[n, :, part], gbuf.at[n, :, part], gsend.at[p, g], grecv.at[n, g], at_n(p)))
+    for g, part in groups:
+        for p in n_peers:
+            copy(gbuf.at[n, :, part], gbuf.at[p, :, part], gsend.at[p, g], grecv.at[p, g], at_n(p)).wait_recv()
+    for c in sent:
+        c.wait_send()
+    out_ref[...] = gbuf[...]
 
 
 def unpack(cap, tab, g_ref, hb_row, out_ref, buf):
@@ -96,6 +172,7 @@
     bw, na = vb // wide, va // narrow
     most = va - (IRREPS - 1) * FEWEST
     cap = most // 2
+    blocks = (CORES, wide // CORES, narrow, ni * bw // narrow, ni * cap)
 
     slab = jnp.sum(
         jnp.where(
@@ -117,28 +194,54 @@
         packed = jnp.minimum(aligned + offset, va - cap)
         tab = jnp.concatenate([slab, occ_part, packed, c_part[:1], c_part[-1:]])
         partial_sums = pl.pallas_call(
-            functools.partial(contract, cap, wide),
-            out_shape=jax.ShapeDtypeStruct((ni * vb, ni * cap), jnp.float32),
+            functools.partial(contract, cap),
+            out_shape=jax.ShapeDtypeStruct(blocks, jnp.float32),
             grid_spec=pltpu.PrefetchScalarGridSpec(
                 num_scalar_prefetch=1,
                 grid=(n_k,),
                 in_specs=[
-                    pl.BlockSpec((ni, 1, va, nc), lambda k, t: (0, k, 0, 0)),
+                    pl.BlockSpec((ni, 1, nc, va), lambda k, t: (0, k, 0, 0)),
                     pl.BlockSpec((1, nc, ni, vb), lambda k, t: (k, 0, 0, 0)),
                     pl.BlockSpec((1, nc), lambda k, t: (0, 0)),
                     pl.BlockSpec((nc, 1), lambda k, t: (0, 0)),
                     pl.BlockSpec((1, vb), lambda k, t: (0, 0)),
                 ],
-                out_specs=pl.BlockSpec((ni * vb, ni * cap), lambda k, t: (0, 0)),
+                out_specs=pl.BlockSpec(blocks, lambda k, t: (0, 0, 0, 0, 0)),
                 scratch_shapes=[
                     pltpu.VMEM((ni, ni * cap, vb), jnp.float32),
+                    pltpu.VMEM((ni, va, nc), jnp.float32),
                     pltpu.VMEM((ni * cap, nc), jnp.float32),
+                    pltpu.VMEM((ni * cap, 3 * nc), jnp.bfloat16),
+                    pltpu.VMEM((ni, 3 * nc, vb), jnp.bfloat16),
                 ],
             ),
             compiler_params=pltpu.CompilerParams(vmem_limit_bytes=60 * 2**20),
-        )(tab, amplitudes, cycle_block, c_part[None, :], c_part[:, None], virtual_irreps[None, :])
-        mine = lax.psum_scatter(partial_sums, ("wide", "narrow"), scatter_dimension=0, tiled=True)
-        summed = lax.all_gather(mine, "narrow", axis=0, tiled=True)
+        )(tab, jnp.swapaxes(amplitudes, 2, 3), cycle_block, c_part[None, :], c_part[:, None], virtual_irreps[None, :])
+        _, zs, _, nr, lanes = blocks
+        groups = lanes // LANES
+        dma = pltpu.SemaphoreType.DMA
+        summed = pl.pallas_call(
+            exchange,
+            out_shape=jax.ShapeDtypeStruct(blocks[2:], jnp.float32),
+            in_specs=[pl.BlockSpec(memory_space=pltpu.VMEM)],
+            out_specs=pl.BlockSpec(memory_space=pltpu.VMEM),
+            scratch_shapes=[
+                pltpu.VMEM(blocks[1:], jnp.float32),
+                pltpu.VMEM(blocks[1:], jnp.float32),
+                pltpu.VMEM((narrow, zs, nr, lanes), jnp.float32),
+                pltpu.VMEM((zs, nr, lanes), jnp.float32),
+                pltpu.VMEM((zs, nr, lanes), jnp.float32),
+                pltpu.VMEM((narrow, nr, lanes), jnp.float32),
+                dma((2, groups)),
+                dma((narrow, groups)),
+                dma((narrow, groups)),
+                dma((zs, groups)),
+                dma((zs, groups)),
+                dma((narrow, groups)),
+                dma((narrow, groups)),
+            ],
+            compiler_params=pltpu.CompilerParams(collective_id=0, has_side_effects=True, vmem_limit_bytes=60 * 2**20),
+        )(partial_sums).reshape(ni * bw, lanes)
         low = jnp.maximum(aligned + offset, starts)
         high = jnp.minimum(aligned + offset + cap, ends)
         tab = jnp.concatenate([slab, packed, low, high, b_part[:1], b_part[-1:], (narrow_pos * na)[None]])

time: 211 us -> 99.2 us (0.47)
  waiting for transfers between devices: 104 us -> 0 us
  Pallas kernels: 48.6 us -> 83.5 us
  local copies, waits for them, and re-layouts: 30.2 us -> 11.6 us
  between operations: 14.1 us -> 0.7 us
  blocking collectives: 11.7 us -> 0 us
    reduce_scatter x1 -> x0, waiting for transfers between devices: 104 us -> none  [part(): lax.psum_scatter(partial_sums, ('wide', 'narrow'), scatter_dimension=0, t...]
    pallas_call x1 -> x2, Pallas kernels: 45.8 us -> 80.7 us  [the longest x1 42.5 us: part(): pl.pallas_call(exchange, out_shape=jax.ShapeDtypeStruct(blocks[2:], jnp.f...]
    unnamed x5 -> x4, local copies, waits for them, and re-layouts: 20.8 us -> 1.05 us
    all_gather x1 -> x0, blocking collectives: 11.7 us -> none  [part(): summed = lax.all_gather(mine, 'narrow', axis=0, tiled=True)]
  transfers between devices with their start and end apart: 1 -> 0, of which waited for: 1 -> 0; matrix products, arithmetic and copies ran while one was open for 2% -> 0% of each run, Pallas kernels for 0% -> 0%
where the time goes in v2:
time: 99.2 us; the launch traced here: 98.2 us
  Pallas kernels  83.5 us (84%)
  local copies, waits for them, and re-layouts  11.6 us (12%)
  other arithmetic  2.44 us (2%)
    pallas_call x1, Pallas kernels, part(): pl.pallas_call(exchange, out_shape=jax.ShapeDtypeStruct(blocks[2:], jnp.f...  42.5 us
    pallas_call x1, Pallas kernels, part(): pl.pallas_call(functools.partial(contract, cap), out_shape=jax.ShapeDtype...  38.2 us
    pallas_call x1, Pallas kernels, part(): pl.pallas_call(functools.partial(unpack, cap), out_shape=jax.ShapeDtypeSt...  2.83 us

profile of v2, /device:TPU:0, one launch (start us, length us, event | category | flops | bytes accessed | tf_op | source)
XLA Modules:
  0.0 98.2 jit_solution(10420370514951427021)
XLA Ops:
  0.0 0.7 dynamic_slice.10
  0.7 0.8 dynamic_slice.11
  1.5 0.8 convert_reduce_fusion
  2.3 0.9 select_reduce_fusion
  3.1 0.1 slice.27
  3.2 0.8 dynamic_slice.9
  4.0 1.3 %dynamic-slice_bitcast_fusion.hb_row = s32[1,80]{1,0:T(1,128)} fusion(s32[640]{0:T(1024)} %param.10, s32[]{:T(128)S(6)} %select_n.20), kind=kLoop, calls=%fused_computation.20 | loop fusion | bytes 644 | tf_op jit(solution)/shard_map/broadcast_in_dim | solution.py:261
  5.3 0.6 fusion.5
  5.9 0.1 add_minimum_fusion.2
  6.0 0.6 fusion.4
  6.6 0.7 pad_add_fusion
  8.0 1.8 %concatenate.17.tab = s32[22]{0:T(128)} concatenate(s32[4]{0:T(128)S(1)} %select_reduce_fusion, s32[8]{0:T(128)S(1)} %dynamic_slice.10, s32[8]{0:T(128)S(1)} %get-tuple-element.62, s32[1]{0:T(128)} %get-tuple-element.58, s32[1]{0:T(128)} %get-tuple-element.57), dimensions={0} | concatenate | bytes 176 | tf_op jit(solution)/shard_map/concatenate | solution.py:195
  9.8 1.8 %concatenate.16.tab = s32[31]{0:T(128)} concatenate(s32[4]{0:T(128)S(1)} %select_reduce_fusion, s32[8]{0:T(128)S(1)} %get-tuple-element.62, s32[8]{0:T(128)S(1)} %get-tuple-element.61, s32[8]{0:T(128)S(1)} %get-tuple-element.46, s32[1]{0:T(128)} %get-tuple-element.64, s32[1]{0:T(128)} %get-tuple-element.63, s32[1]{0:T(128)} %bitcast.6), dimensions={0} | concatenate | bytes 248 | tf_op jit(solution)/shard_map/concatenate | solution.py:247
  11.6 1.3 %broadcast_in_dim.52.hb_row = s32[1,640]{1,0:T(1,128)} reshape(s32[640]{0:T(1024)} %param.10) | data formatting | bytes 5120 | tf_op jit(solution)/shard_map/broadcast_in_dim | solution.py:189
  12.9 0.8 copy.11.hc_col
  13.6 38.2 %shard_map.57.q_ref = f32[2,4,4,80,384]{4,3,2,1,0:T(8,128)} custom-call(s32[22]{0:T(128)} %concatenate.17.tab, f32[4,8,160,640]{3,2,1,0:T(8,128)} %bitcast.13, f32[8,160,4,640]{3,2,1,0:T(4,128)} %w_ref.1, s32[1,160]{1,0:T(1,128)S(1)} %bitcast.18, s32[160,1]{1,0:T(8,128)} %copy.11.hc_col, s32[1,640]{1,0:T(1,128)} %broadcast_in_dim.52.hb_row), custom_call_target="tpu_custom_call" | custom-call | tf_op jit(solution)/shard_map/pallas_call | solution.py:196
  51.8 0.0 copy-start.1
  51.8 42.5 %shard_map.58 = f32[4,80,384]{2,1,0:T(8,128)} custom-call(f32[2,4,4,80,384]{4,3,2,1,0:T(8,128)} %shard_map.57.q_ref), custom_call_target="tpu_custom_call" | custom-call | tf_op jit(solution)/shard_map/pallas_call | solution.py:223
  94.3 2.8 %shard_map.59 = f32[4,4,160,80]{3,2,1,0:T(8,128)S(1)} custom-call(s32[31]{0:T(128)} %concatenate.16.tab, f32[320,384]{1,0:T(8,128)} %bitcast.15, s32[1,80]{1,0:T(1,128)} %dynamic-slice_bitcast_fusion.hb_row), custom_call_target="tpu_custom_call" | custom-call | tf_op jit(solution)/shard_map/pallas_call | solution.py:248
  97.1 0.0 copy-done.1
  97.2 0.0 copy-start
  97.2 1.0 %copy-done = f32[4,4,160,80]{3,2,1,0:T(8,128)} copy-done((f32[4,4,160,80]{3,2,1,0:T(8,128)}, f32[4,4,160,80]{3,2,1,0:T(8,128)S(1)}, u32[]{:S(2)}) %copy-start) | copy-done | bytes 819224
  (1 shorter events, 0.0 us)
Async XLA Ops:
  51.8 45.3 %copy-start.1 = (s32[640]{0:T(1024)S(1)}, s32[640]{0:T(1024)}, u32[]{:S(2)}) copy-start(s32[640]{0:T(1024)} %param.10) | copy-start | bytes 7684
  97.2 1.1 %copy-start = (f32[4,4,160,80]{3,2,1,0:T(8,128)}, f32[4,4,160,80]{3,2,1,0:T(8,128)S(1)}, u32[]{:S(2)}) copy-start(f32[4,4,160,80]{3,2,1,0:T(8,128)S(1)} %get-tuple-element.67) | copy-start | bytes 2457604

commit v3 on v2

--- a/solution.py
+++ b/solution.py
@@ -24,49 +24,62 @@
     return jnp.dot(x, y, preferred_element_type=jnp.float32)
 
 
-def contract(cap, tab, a_ref, w_ref, hc_row, hc_col, hb_row, out_ref, acc, turn, rows, deep_l, deep_w):
+def label_of(at, starts):
+    return sum((at >= starts[h]).astype(jnp.int32) for h in range(1, IRREPS))
+
+
+def label_at(at, starts):
+    return sum(jnp.where(at >= starts[h], 1, 0) for h in range(1, IRREPS))
+
+
+def contract(cap, offset, starts, occupied, slab, a_ref, w_ref, out_ref, acc, turn, rows, deep_l, deep_w, labels, c_labels):
     k = pl.program_id(0)
     n_k = pl.num_programs(0)
-    ni, nc = a_ref.shape[0], a_ref.shape[2]
+    ni, nc, va = a_ref.shape[0], a_ref.shape[2], a_ref.shape[3]
     cores, zs, narrow, nr, _ = out_ref.shape
-    hk = tab[ni + k]
-    base = ni + n_k
-    first, last = tab[base + IRREPS], tab[base + IRREPS + 1]
-    c_labels = hc_row[...]
+    c0 = lax.axis_index("narrow") * nc
+    hk = occupied[lax.axis_index("wide") * n_k + k]
+    slab_irreps = [occupied[slab[i]] for i in range(ni)]
+    first, last = label_at(c0, starts), label_at(c0 + nc - 1, starts)
+
+    @pl.when(k == 0)
+    def _():
+        acc[...] = jnp.zeros_like(acc)
+        rows[...] = jnp.zeros_like(rows)
+        c_labels[...] = label_of(c0 + lax.broadcasted_iota(jnp.int32, c_labels.shape, 1), starts)
+        labels[...] = label_of(c0 + lax.broadcasted_iota(jnp.int32, labels.shape, 0), starts) ^ label_of(
+            lax.broadcasted_iota(jnp.int32, labels.shape, 1), starts
+        )
+
     for i in range(ni):
-        g = tab[i] ^ hk
         turn[i] = a_ref[i, 0].T
 
-        def pick(h, kept):
-            start = pl.multiple_of(tab[base + (h ^ g)], ROWS)
-            return jnp.where(c_labels == h, turn[i, pl.ds(start, cap), :], kept)
-
-        rows[i * cap : (i + 1) * cap, :] = lax.fori_loop(first, last + 1, pick, jnp.zeros((cap, nc), jnp.float32))
+    def pick(h, carry):
+        mine = c_labels[...] == h
+        for i in range(ni):
+            block = h ^ slab_irreps[i] ^ hk
+            start = pl.multiple_of(jnp.minimum(starts[block] // ROWS * ROWS + offset, va - cap), ROWS)
+            at = slice(i * cap, (i + 1) * cap)
+            rows[at, :] = jnp.where(mine, turn[i, pl.ds(start, cap), :], rows[at, :])
+        return carry
+
+    lax.fori_loop(first, last + 1, pick, 0)
     l_hi, l_lo = split(rows[...])
     joined = nc % 16 == 0
     if joined:
         deep_l[:, :nc] = l_hi
         deep_l[:, nc : 2 * nc] = l_hi
         deep_l[:, 2 * nc :] = l_lo
-    labels = hc_col[...] ^ hb_row[...]
     w_all = jnp.swapaxes(w_ref[0], 0, 1)
     for j in range(ni):
-        w_hi, w_lo = split(jnp.where(labels == (tab[j] ^ hk), w_all[j], 0.0))
+        w_hi, w_lo = split(jnp.where(labels[...] == (slab_irreps[j] ^ hk), w_all[j], 0.0))
         if joined:
             deep_w[j, :nc] = w_hi
             deep_w[j, nc : 2 * nc] = w_lo
             deep_w[j, 2 * nc :] = w_hi
-            term = mm(deep_l[...], deep_w[j])
+            acc[j] += mm(deep_l[...], deep_w[j])
         else:
-            term = mm(l_hi, w_hi) + mm(l_hi, w_lo) + mm(l_lo, w_hi)
-
-        @pl.when(k == 0)
-        def _():
-            acc[j] = term
-
-        @pl.when(k > 0)
-        def _():
-            acc[j] += term
+            acc[j] += mm(l_hi, w_hi) + mm(l_hi, w_lo) + mm(l_lo, w_hi)
 
     @pl.when(k == n_k - 1)
     def _():
@@ -142,22 +155,28 @@
     out_ref[...] = gbuf[...]
 
 
-def unpack(cap, tab, g_ref, hb_row, out_ref, buf):
+def unpack(cap, offset, starts, occupied, slab, g_ref, out_ref, buf):
     ni, _, na, bw = out_ref.shape
+    va = na * lax.axis_size("narrow")
     buf[...] = jnp.zeros_like(buf)
-    first, last, a0 = (tab[ni + 3 * IRREPS + n] for n in range(3))
-    labels = hb_row[...]
+    slab_irreps = [occupied[slab[i]] for i in range(ni)]
+    a0, b0 = lax.axis_index("narrow") * na, lax.axis_index("wide") * bw
+    first, last = label_at(b0, starts), label_at(b0 + bw - 1, starts)
+    labels = label_of(b0 + lax.broadcasted_iota(jnp.int32, (1, bw), 1), starts)
     at = a0 + lax.broadcasted_iota(jnp.int32, (na, bw), 0)
     for j in range(ni):
         turned = g_ref[j * bw : (j + 1) * bw, :].T
         for i in range(ni):
             buf[na : na + cap, :] = turned[i * cap : (i + 1) * cap]
-            g = tab[i] ^ tab[j]
+            g = slab_irreps[i] ^ slab_irreps[j]
 
             def place(h, kept):
                 block = h ^ g
-                start = jnp.clip(na + a0 - tab[ni + block], 0, na + cap)
-                low, high = tab[ni + IRREPS + block], tab[ni + 2 * IRREPS + block]
+                aligned = starts[block] // ROWS * ROWS + offset
+                low = jnp.maximum(aligned, starts[block])
+                end = jnp.where(block == IRREPS - 1, va, starts[jnp.minimum(block + 1, IRREPS - 1)])
+                high = jnp.minimum(aligned + cap, end)
+                start = jnp.clip(na + a0 - jnp.minimum(aligned, va - cap), 0, na + cap)
                 use = (labels == h) & (at >= low) & (at < high)
                 return jnp.where(use, buf[pl.ds(pl.multiple_of(start, ROWS), na), :], kept)
 
@@ -168,55 +187,40 @@
     ni, n_k, va, nc = amplitudes.shape
     vb = cycle_block.shape[3]
     wide, narrow = lax.axis_size("wide"), lax.axis_size("narrow")
-    wide_pos, narrow_pos = lax.axis_index("wide"), lax.axis_index("narrow")
     bw, na = vb // wide, va // narrow
     most = va - (IRREPS - 1) * FEWEST
     cap = most // 2
     blocks = (CORES, wide // CORES, narrow, ni * bw // narrow, ni * cap)
 
-    slab = jnp.sum(
-        jnp.where(
-            jnp.arange(occupied_irreps.shape[0], dtype=jnp.int32)[None, :] == slab_orbitals[:, None],
-            occupied_irreps[None, :],
-            0,
-        ),
-        axis=1,
-    )
-    occ_part = lax.dynamic_slice_in_dim(occupied_irreps, wide_pos * n_k, n_k)
-    c_part = lax.dynamic_slice_in_dim(virtual_irreps, narrow_pos * nc, nc)
-    b_part = lax.dynamic_slice_in_dim(virtual_irreps, wide_pos * bw, bw)
     names = jnp.arange(IRREPS, dtype=jnp.int32)
     starts = jnp.sum((virtual_irreps[None, :] < names[:, None]).astype(jnp.int32), axis=1)
     aligned = starts // ROWS * ROWS
     ends = jnp.concatenate([starts[1:], jnp.full((1,), va, jnp.int32)])
 
     def part(offset):
-        packed = jnp.minimum(aligned + offset, va - cap)
-        tab = jnp.concatenate([slab, occ_part, packed, c_part[:1], c_part[-1:]])
         partial_sums = pl.pallas_call(
-            functools.partial(contract, cap),
+            functools.partial(contract, cap, offset),
             out_shape=jax.ShapeDtypeStruct(blocks, jnp.float32),
             grid_spec=pltpu.PrefetchScalarGridSpec(
-                num_scalar_prefetch=1,
+                num_scalar_prefetch=3,
                 grid=(n_k,),
                 in_specs=[
-                    pl.BlockSpec((ni, 1, nc, va), lambda k, t: (0, k, 0, 0)),
-                    pl.BlockSpec((1, nc, ni, vb), lambda k, t: (k, 0, 0, 0)),
-                    pl.BlockSpec((1, nc), lambda k, t: (0, 0)),
-                    pl.BlockSpec((nc, 1), lambda k, t: (0, 0)),
-                    pl.BlockSpec((1, vb), lambda k, t: (0, 0)),
+                    pl.BlockSpec((ni, 1, nc, va), lambda k, *t: (0, k, 0, 0)),
+                    pl.BlockSpec((1, nc, ni, vb), lambda k, *t: (k, 0, 0, 0)),
                 ],
-                out_specs=pl.BlockSpec(blocks, lambda k, t: (0, 0, 0, 0, 0)),
+                out_specs=pl.BlockSpec(blocks, lambda k, *t: (0, 0, 0, 0, 0)),
                 scratch_shapes=[
                     pltpu.VMEM((ni, ni * cap, vb), jnp.float32),
                     pltpu.VMEM((ni, va, nc), jnp.float32),
                     pltpu.VMEM((ni * cap, nc), jnp.float32),
                     pltpu.VMEM((ni * cap, 3 * nc), jnp.bfloat16),
                     pltpu.VMEM((ni, 3 * nc, vb), jnp.bfloat16),
+                    pltpu.VMEM((nc, vb), jnp.int32),
+                    pltpu.VMEM((1, nc), jnp.int32),
                 ],
             ),
             compiler_params=pltpu.CompilerParams(vmem_limit_bytes=60 * 2**20),
-        )(tab, jnp.swapaxes(amplitudes, 2, 3), cycle_block, c_part[None, :], c_part[:, None], virtual_irreps[None, :])
+        )(starts, occupied_irreps, slab_orbitals, jnp.swapaxes(amplitudes, 2, 3), cycle_block)
         _, zs, _, nr, lanes = blocks
         groups = lanes // LANES
         dma = pltpu.SemaphoreType.DMA
@@ -242,23 +246,19 @@
             ],
             compiler_params=pltpu.CompilerParams(collective_id=0, has_side_effects=True, vmem_limit_bytes=60 * 2**20),
         )(partial_sums).reshape(ni * bw, lanes)
-        low = jnp.maximum(aligned + offset, starts)
-        high = jnp.minimum(aligned + offset + cap, ends)
-        tab = jnp.concatenate([slab, packed, low, high, b_part[:1], b_part[-1:], (narrow_pos * na)[None]])
         return pl.pallas_call(
-            functools.partial(unpack, cap),
+            functools.partial(unpack, cap, offset),
             out_shape=jax.ShapeDtypeStruct((ni, ni, na, bw), jnp.float32),
             grid_spec=pltpu.PrefetchScalarGridSpec(
-                num_scalar_prefetch=1,
+                num_scalar_prefetch=3,
                 grid=(1,),
                 in_specs=[
-                    pl.BlockSpec((ni * bw, ni * cap), lambda k, t: (0, 0)),
-                    pl.BlockSpec((1, bw), lambda k, t: (0, 0)),
+                    pl.BlockSpec((ni * bw, ni * cap), lambda k, *t: (0, 0)),
                 ],
-                out_specs=pl.BlockSpec((ni, ni, na, bw), lambda k, t: (0, 0, 0, 0)),
+                out_specs=pl.BlockSpec((ni, ni, na, bw), lambda k, *t: (0, 0, 0, 0)),
                 scratch_shapes=[pltpu.VMEM((2 * na + cap, bw), jnp.float32)],
             ),
-        )(tab, summed, b_part[None, :])
+        )(starts, occupied_irreps, slab_orbitals, summed)
 
     first = part(0)
     return lax.cond(jnp.max(ends - aligned) > cap, lambda x: x + part(cap), lambda x: x, first)

time: 99.2 us -> 76.3 us (0.77)
  Pallas kernels: 83.5 us -> 72.8 us
  local copies, waits for them, and re-layouts: 11.6 us -> 1.13 us
    pallas_call x2, Pallas kernels: 41 us -> 30.5 us  [the longest x1 27.2 us: part(): pl.pallas_call(functools.partial(contract, cap, offset), out_shape=jax.Sh...]
    concatenate x2 -> x0, local copies, waits for them, and re-layouts: 3.65 us -> none  [the longest x1 1.85 us: part(): jnp.concatenate([slab, packed, low, high, b_part[:1], b_part[-1:], (narro...]
    broadcast_in_dim x3 -> x0, local copies, waits for them, and re-layouts: 3.34 us -> none  [the longest x1 1.3 us: part(): b_part[None, :]]
    dynamic_slice x3 -> x0, local copies, waits for them, and re-layouts: 2.25 us -> none  [the longest x1 0.76 us: local(): b_part = lax.dynamic_slice_in_dim(virtual_irreps, wide_pos * bw, bw)]
    slice x2 -> x0, local copies, waits for them, and re-layouts: 1.23 us -> none  [the longest x1 0.65 us: part(): b_part[-1:]]
where the time goes in v3:
time: 76.3 us; the launch traced here: 76.2 us
  Pallas kernels  72.8 us (95%)
  other arithmetic  1.51 us (2%)
  local copies, waits for them, and re-layouts  1.13 us (1%)
    pallas_call x1, Pallas kernels, part(): pl.pallas_call(exchange, out_shape=jax.ShapeDtypeStruct(blocks[2:], jnp.f...  42.3 us
    pallas_call x1, Pallas kernels, part(): pl.pallas_call(functools.partial(contract, cap, offset), out_shape=jax.Sh...  27.2 us
    pallas_call x1, Pallas kernels, part(): pl.pallas_call(functools.partial(unpack, cap, offset), out_shape=jax.Shap...  3.33 us

profile of v3, /device:TPU:0, one launch (start us, length us, event | category | flops | bytes accessed | tf_op | source)
XLA Modules:
  0.0 76.2 jit_solution(4267570980213173932)
XLA Ops:
  0.0 0.8 %convert_reduce_fusion.starts = s32[8]{0:T(128)S(1)} fusion(s32[640]{0:T(1024)} %param.10), kind=kLoop, calls=%fused_computation | loop fusion | flops 15352 | bytes 2592 | tf_op jit(solution)/shard_map/reduce_sum | solution.py:196
  0.8 0.1 slice.3
  0.9 0.7 fusion
  2.2 27.2 %shard_map.57.q_ref = f32[2,4,4,80,384]{4,3,2,1,0:T(8,128)} custom-call(s32[8]{0:T(128)S(1)} %convert_reduce_fusion.starts, s32[64]{0:T(128)} %occupied.3, s32[4]{0:T(128)} %slab.3, f32[4,8,160,640]{3,2,1,0:T(8,128)} %bitcast.4, f32[8,160,4,640]{3,2,1,0:T(4,128)} %w_ref.1), custom_call_target="tpu_custom_call" | custom-call | tf_op jit(solution)/shard_map/pallas_call | solution.py:201
  29.5 0.0 copy-start.1
  29.5 0.0 copy-start.2
  29.5 42.3 %shard_map.58 = f32[4,80,384]{2,1,0:T(8,128)} custom-call(f32[2,4,4,80,384]{4,3,2,1,0:T(8,128)} %shard_map.57.q_ref), custom_call_target="tpu_custom_call" | custom-call | tf_op jit(solution)/shard_map/pallas_call | solution.py:227
  71.8 0.0 copy-done.1
  71.8 0.0 copy-done.2
  71.8 3.3 %shard_map.59 = f32[4,4,160,80]{3,2,1,0:T(8,128)S(1)} custom-call(s32[8]{0:T(128)S(1)} %convert_reduce_fusion.starts, s32[64]{0:T(128)S(1)} %copy-done.1, s32[4]{0:T(128)S(1)} %copy-done.2, f32[320,384]{1,0:T(8,128)} %bitcast.6), custom_call_target="tpu_custom_call" | custom-call | tf_op jit(solution)/shard_map/pallas_call | solution.py:249
  75.1 0.0 copy-start
  75.1 1.0 %copy-done = f32[4,4,160,80]{3,2,1,0:T(8,128)} copy-done((f32[4,4,160,80]{3,2,1,0:T(8,128)}, f32[4,4,160,80]{3,2,1,0:T(8,128)S(1)}, u32[]{:S(2)}) %copy-start) | copy-done | bytes 819224
  (1 shorter events, 0.0 us)
Async XLA Ops:
  29.5 42.3 %copy-start.1 = (s32[64]{0:T(128)S(1)}, s32[64]{0:T(128)}, u32[]{:S(2)}) copy-start(s32[64]{0:T(128)} %occupied.3) | copy-start | bytes 772
  29.5 42.3 %copy-start.2 = (s32[4]{0:T(128)S(1)}, s32[4]{0:T(128)}, u32[]{:S(2)}) copy-start(s32[4]{0:T(128)} %slab.3) | copy-start | bytes 52
  75.1 1.1 %copy-start = (f32[4,4,160,80]{3,2,1,0:T(8,128)}, f32[4,4,160,80]{3,2,1,0:T(8,128)S(1)}, u32[]{:S(2)}) copy-start(f32[4,4,160,80]{3,2,1,0:T(8,128)S(1)} %get-tuple-element.30) | copy-start | bytes 2457604
